TPU v7x, 1024 devices: a whole 4x8x16 slice. The times are simulated.
1024 devices in a mesh: dp: 8 (over y), ctx: 64 (over z, x), tensor: 2 (over core).
Axes of the slice: x: 4, y: 8, z: 16, core: 2. Of those that a mesh axis runs over, the one named last changes fastest.
Arguments:
- x_seq: bfloat16 [8, 8192, 2048], P('dp', 'ctx', 'tensor'), may hold values from -6 to 6
- dt_seq: float32 [8, 32, 8192], P('dp', 'tensor', 'ctx'), may hold values from 0.05 to 0.5
- b_seq: bfloat16 [8, 8192, 128], P('dp', 'ctx'), may hold values from -2 to 2
- c_seq: bfloat16 [8, 8192, 128], P('dp', 'ctx'), may hold values from -2 to 2
- dy_seq: bfloat16 [8, 8192, 2048], P('dp', 'ctx', 'tensor'), may hold values from -6 to 6
- saved_states: float32 [8, 64, 2048, 128], P('dp', 'ctx', 'tensor'), may hold values from -4 to 4
- doc_starts: int32 [8, 8192], P('dp', 'ctx'), may hold values 0 or 1
- decay_rates: float32 [32], P('tensor'), may hold values from 0.0005 to 0.2
Outputs:
- grad_x: bfloat16 [8, 8192, 2048], P('dp', 'ctx', 'tensor')
- grad_dt: float32 [8, 32, 8192], P('dp', 'tensor', 'ctx')
- grad_b: float32 [8, 8192, 128], P('dp', 'ctx')
- grad_c: float32 [8, 8192, 128], P('dp', 'ctx')
- grad_rates: float32 [8, 32], P('dp', 'tensor')
Inputs may be any that keep to these rules, and one draw needn't show every extreme that they name: `doc_starts`: 1 marks the first position of a document; the state restarts there.
All inputs are finite; a program needn't handle non-finite values. No bound on the sum of `doc_starts` on one device may be relied on, other than what follows from the above.
Results may differ from a plain program's by a relative error of at most 0.001.
Values sent between devices are 32-bit elements; how exact they have to be, the bound alone decides.
No kernel may reach another device: no remote copies, remote signals or barrier semaphores. Data moves between devices by JAX's collectives and lax.ppermute only.
A program may use at most 128 MiB of HBM per device.

v0:
```python
import jax
import jax.numpy as jnp
from jax import lax
from jax.sharding import PartitionSpec as P

BLK = 64


HIGHEST_PREC = lax.Precision.HIGHEST


def carried_in(x, axis, combine, identity):
    size, position = (lax.axis_size(axis), lax.axis_index(axis))
    everything = jax.tree.map(lambda part: lax.all_gather(part, axis), x)
    start = jax.tree.map(
        lambda part, zero: jnp.broadcast_to(jnp.asarray(zero, part.dtype), part.shape), x, identity
    )

    def step(k, before):
        at = size - 1 - k
        reached = at > position
        new = combine(before, jax.tree.map(lambda part: part[at], everything))
        return jax.tree.map(lambda a, b: jnp.where(reached, a, b), new, before)

    return lax.fori_loop(0, size, step, start)


def edge_parts(dt_blk, start_blk, rates_blk):
    log_step = -dt_blk * rates_blk[:, None]
    log_cum = jnp.cumsum(log_step, axis=1)
    doc_count = jnp.cumsum(start_blk, axis=0)
    entry_dec = jnp.where(doc_count[None, :] == 0, jnp.exp(log_cum), 0.0)
    tail_dec = jnp.where(
        doc_count[None, :] == doc_count[-1], jnp.exp(log_cum[:, -1:] - log_cum), 0.0
    )
    return (log_cum, doc_count, entry_dec, tail_dec)


def decay_parts(dt_blk, start_blk, rates_blk):
    log_cum, doc_count, entry_dec, tail_dec = edge_parts(dt_blk, start_blk, rates_blk)
    block_len = start_blk.shape[0]
    row_idx = lax.broadcasted_iota(jnp.int32, (block_len, block_len), 0)
    col_idx = lax.broadcasted_iota(jnp.int32, (block_len, block_len), 1)
    below = row_idx >= col_idx
    same_doc = below & (doc_count[:, None] == doc_count[None, :])
    spread = jnp.where(same_doc[None], log_cum[:, :, None] - log_cum[:, None, :], -1e30)
    decay_mat = jnp.exp(spread)
    lower_tri = below.astype(dt_blk.dtype)
    return (decay_mat, entry_dec, tail_dec, lower_tri)


def advance(x_blk, dt_blk, b_blk, start_blk, rates_blk, h_init):
    _, _, entry_dec, tail_dec = edge_parts(dt_blk, start_blk, rates_blk)
    step_in = dt_blk[:, :, None] * x_blk
    return entry_dec[:, -1][:, None, None] * h_init + jnp.einsum(
        "hs,hsp,sn->hpn", tail_dec, step_in, b_blk, precision=HIGHEST_PREC
    )


def block_grads(x_blk, dt_blk, b_blk, c_blk, dy_blk, start_blk, rates_blk, h_init, incoming):
    decay_mat, entry_dec, tail_dec, lower_tri = decay_parts(dt_blk, start_blk, rates_blk)
    last_dec = entry_dec[:, -1]
    step_in = dt_blk[:, :, None] * x_blk
    c_dot_b = jnp.dot(c_blk, b_blk.T, precision=HIGHEST_PREC)
    dy_dot_s = jnp.einsum("hup,hsp->hus", dy_blk, step_in, precision=HIGHEST_PREC)
    weight_mat = decay_mat * dy_dot_s
    dy_state = jnp.einsum("htp,hpn->htn", dy_blk, h_init, precision=HIGHEST_PREC)
    grad_cpart = jnp.einsum("hts,sn->tn", weight_mat, b_blk, precision=HIGHEST_PREC) + jnp.einsum(
        "ht,htn->tn", entry_dec, dy_state, precision=HIGHEST_PREC
    )
    mix_mat = decay_mat * c_dot_b[None]
    f_dot_b = jnp.einsum("tn,hpn->htp", b_blk, incoming, precision=HIGHEST_PREC)
    grad_s = (
        jnp.einsum("hut,hup->htp", mix_mat, dy_blk, precision=HIGHEST_PREC)
        + tail_dec[:, :, None] * f_dot_b
    )
    s_dot_f = jnp.einsum("htp,hpn->htn", step_in, incoming, precision=HIGHEST_PREC)
    grad_bpart = jnp.einsum("hut,un->tn", weight_mat, c_blk, precision=HIGHEST_PREC) + jnp.einsum(
        "ht,htn->tn", tail_dec, s_dot_f, precision=HIGHEST_PREC
    )
    kernel_mat = weight_mat * c_dot_b[None]
    prefix_mat = jnp.einsum("hus,ts->hut", kernel_mat, lower_tri, precision=HIGHEST_PREC)
    first_term = jnp.sum(lower_tri[None] * prefix_mat, axis=1)
    q_term = jnp.sum(dy_state * c_blk[None], axis=2)
    second_term = jnp.einsum("hu,ut->ht", entry_dec * q_term, lower_tri, precision=HIGHEST_PREC)
    p_term = jnp.sum(step_in * f_dot_b, axis=2)
    third_term = jnp.einsum("hs,ts->ht", tail_dec * p_term, lower_tri, precision=HIGHEST_PREC)
    fourth_term = last_dec * jnp.sum(incoming * h_init, axis=(1, 2))
    summed = first_term + second_term + third_term + fourth_term[:, None]
    scaled = summed - jnp.sum(grad_s * step_in, axis=2)
    grad_dtpart = jnp.sum(x_blk * grad_s, axis=2) - rates_blk[:, None] * scaled
    grad_xpart = dt_blk[:, :, None] * grad_s
    grad_rpart = -jnp.sum(dt_blk * scaled, axis=1)
    outgoing = (
        jnp.einsum("hu,hup,un->hpn", entry_dec, dy_blk, c_blk, precision=HIGHEST_PREC)
        + last_dec[:, None, None] * incoming
    )
    return (grad_xpart, grad_dtpart, grad_bpart, grad_cpart, grad_rpart, outgoing)


def split_blocks(x_loc, dt_loc, b_loc, c_loc, dy_loc, start_loc):
    tok_count, num_heads, head_dim = x_loc.shape
    num_blocks = tok_count // BLK
    x_parts = x_loc.reshape(num_blocks, BLK, num_heads, head_dim).transpose(0, 2, 1, 3)
    dy_parts = dy_loc.reshape(num_blocks, BLK, num_heads, head_dim).transpose(0, 2, 1, 3)
    dt_parts = dt_loc.reshape(num_heads, num_blocks, BLK).transpose(1, 0, 2)
    b_parts = b_loc.reshape(num_blocks, BLK, b_loc.shape[1])
    c_parts = c_loc.reshape(num_blocks, BLK, c_loc.shape[1])
    st_parts = start_loc.reshape(num_blocks, BLK)
    return (x_parts, dt_parts, b_parts, c_parts, dy_parts, st_parts)


def device_grads(x_loc, dt_loc, b_loc, c_loc, dy_loc, start_loc, rates_loc, h_first, incoming):
    x_parts, dt_parts, b_parts, c_parts, dy_parts, st_parts = split_blocks(
        x_loc, dt_loc, b_loc, c_loc, dy_loc, start_loc
    )

    def forward(h_now, pieces):
        x_one, dt_one, b_one, st_one = pieces
        return (advance(x_one, dt_one, b_one, st_one, rates_loc, h_now), h_now)

    _, h_starts = lax.scan(forward, h_first, (x_parts, dt_parts, b_parts, st_parts))

    def device_backward(carried, pieces):
        x_one, dt_one, b_one, c_one, dy_one, st_one, h_one = pieces
        results = block_grads(
            x_one, dt_one, b_one, c_one, dy_one, st_one, rates_loc, h_one, carried
        )
        return (results[5], results[:5])

    final, grads = lax.scan(
        device_backward,
        incoming,
        (x_parts, dt_parts, b_parts, c_parts, dy_parts, st_parts, h_starts),
        reverse=True,
    )
    dx_parts, ddt_parts, db_parts, dc_parts, dr_parts = grads
    dx_local = dx_parts.transpose(0, 2, 1, 3).reshape(x_loc.shape)
    ddt_local = ddt_parts.transpose(1, 0, 2).reshape(dt_loc.shape)
    db_local = db_parts.reshape(b_loc.shape)
    dc_local = dc_parts.reshape(c_loc.shape)
    return (dx_local, ddt_local, db_local, dc_local, jnp.sum(dr_parts, axis=0), final)


def chain_acc(x_loc, dt_loc, b_loc, c_loc, dy_loc, start_loc, rates_loc):
    _, dt_parts, _, c_parts, dy_parts, st_parts = split_blocks(
        x_loc, dt_loc, b_loc, c_loc, dy_loc, start_loc
    )

    def chain_backward(carried, pieces):
        dt_one, c_one, dy_one, st_one = pieces
        _, _, entry_dec, _ = edge_parts(dt_one, st_one, rates_loc)
        outgoing = (
            jnp.einsum("hu,hup,un->hpn", entry_dec, dy_one, c_one, precision=HIGHEST_PREC)
            + entry_dec[:, -1][:, None, None] * carried
        )
        return (outgoing, None)

    empty = jnp.zeros((x_loc.shape[1], x_loc.shape[2], b_loc.shape[1]), jnp.float32)
    final, _ = lax.scan(
        chain_backward, empty, (dt_parts, c_parts, dy_parts, st_parts), reverse=True
    )
    return final


def block_decay(dt_loc, start_loc, rates_loc):
    return jnp.where(jnp.sum(start_loc) == 0, jnp.exp(-rates_loc * jnp.sum(dt_loc, axis=1)), 0.0)


def pass_chain(whole_dec, local_acc):

    def compose(early_map, later_map):
        return (
            later_map[0] * early_map[0],
            later_map[1] + later_map[0][:, None, None] * early_map[1],
        )

    identity_map = (jnp.ones_like(whole_dec), jnp.zeros_like(local_acc))
    _, carried = carried_in((whole_dec, local_acc), "ctx", compose, identity_map)
    return carried


def per_device(x_seq, dt_seq, b_seq, c_seq, dy_seq, saved_states, doc_starts, decay_rates):
    num_heads = decay_rates.shape[0]
    tok_count = x_seq.shape[1]
    head_dim = x_seq.shape[2] // num_heads
    x_loc = x_seq[0].astype(jnp.float32).reshape(tok_count, num_heads, head_dim)
    dy_loc = dy_seq[0].astype(jnp.float32).reshape(tok_count, num_heads, head_dim)
    dt_loc = dt_seq[0]
    b_loc = b_seq[0].astype(jnp.float32)
    c_loc = c_seq[0].astype(jnp.float32)
    start_loc = doc_starts[0]
    h_first = saved_states[0, 0].reshape(num_heads, head_dim, b_loc.shape[1])
    whole_dec = block_decay(dt_loc, start_loc, decay_rates)
    local_acc = chain_acc(x_loc, dt_loc, b_loc, c_loc, dy_loc, start_loc, decay_rates)
    carried = pass_chain(whole_dec, local_acc)
    dx_local, ddt_local, db_local, dc_local, drate_local, _ = device_grads(
        x_loc, dt_loc, b_loc, c_loc, dy_loc, start_loc, decay_rates, h_first, carried
    )
    db_sum, dc_sum = lax.psum((db_local, dc_local), "tensor")
    drate_sum = lax.psum(drate_local, "ctx")
    return (
        dx_local.astype(jnp.bfloat16).reshape(1, tok_count, num_heads * head_dim),
        ddt_local[None],
        db_sum[None],
        dc_sum[None],
        drate_sum[None],
    )


def solution(mesh):
    placed = (
        P("dp", "ctx", "tensor"),
        P("dp", "tensor", "ctx"),
        P("dp", "ctx", None),
        P("dp", "ctx", None),
        P("dp", "ctx", "tensor"),
        P("dp", "ctx", "tensor", None),
        P("dp", "ctx"),
        P("tensor"),
    )
    return jax.shard_map(
        per_device,
        mesh=mesh,
        in_specs=placed,
        out_specs=(
            P("dp", "ctx", "tensor"),
            P("dp", "tensor", "ctx"),
            P("dp", "ctx", None),
            P("dp", "ctx", None),
            P("dp", "tensor"),
        ),
        check_vma=False,
    )
```

profile of v0, /device:TPU:56, one launch (start us, length us, event | category | flops | bytes accessed | tf_op | source)
XLA Modules:
  0.0 592.9 jit_solution(7637735550893746320)
XLA Ops:
  8.8 1.9 fusion.77
  11.6 1.2 reshape.284
  14.0 4.6 while.69
  21.0 1.3 dynamic-slice
  23.7 158.5 %all-reduce = f32[1024]{0:T(1024)S(1)} all-reduce(f32[1024]{0:T(1024)S(1)} %fusion.76), channel_id=3, replica_groups=mesh['dp'=8,'ctx'=64,'tensor'=2] {'ctx'}, use_global_device_ids=true, to_apply=%add | all-reduce | flops 1024 | bytes 8192
  182.3 2.2 reshape.285
  184.6 1.6 copy.52
  187.0 11.2 %while.67 = (s32[]{:T(128)}, f32[16,64,128]{2,1,0:T(8,128)S(1)}, f32[2,16,64,128]{3,2,1,0:T(8,128)}, s32[2,64]{1,0:T(2,128)S(1)}, f32[2,16,64]{2,1,0:T(8,128)S(1...) while((s32[]{:T(128)}, f32[16,64,128]{2,1,0:T(8,128)S(1)}, ...), condition=%wide.region_11.12_spmd, body=%wide.region_8.11_spmd.sunk | while | flops 101129296 | bytes 2703756 | solution.py:122
  198.2 129.8 %all-gather.4.cloned.1.call-done = f32[1024,64,128]{2,1,0:T(8,128)} async-done(((f32[16,64,128]{2,1,0:T(8,128)}), f32[1024,64,128]{2,1,0:T(8,128)}) %all-gather.4.cloned.1.call-update) | async-done | bytes 33554448 | tf_op jit(solution)/shard_map/all_gather | solution.py:14
  327.9 78.5 %while.70 = (s32[]{:T(128)}, f32[16,64,128]{2,1,0:T(8,128)S(1)}, s32[]{:T(128)}, f32[64,16,64,128]{3,2,1,0:T(8,128)}, f32[64,16]{1,0:T(8,128)S(1)}, /*index=5*/s32[]{:T(128)}, s32[]{:T(128)}, s32[]{:T(128)}, s32[]{:T(128)}) while((s32[]{:T(128)}, f32[16,64,128]{2,1,0:T(8,128)S(1)}, s32[]{:T(128)}, f32[64,16,64,128]{3,2,1,0:T(8,128)}, ...), condition=%wide.region_7.8_spmd.clone, body=%wide.region_6.7_spmd.clone.sunk | while | flops 524296 | bytes 1573223 | solution.py:25
  330.4 1.2 fusion.150
  331.6 1.2 fusion.150
  332.8 1.2 fusion.150
  407.4 31.8 %while.68 = (s32[]{:T(128)}, f32[16,64,128]{2,1,0:T(8,128)S(1)}, bf16[2,16,64,64]{2,3,1,0:T(8,128)(2,1)}, f32[2,16,64]{2,1,0:T(8,128)S(1)}, f32[2,64,128]{2,1,0:...) while((s32[]{:T(128)}, f32[16,64,128]{2,1,0:T(8,128)S(1)}, ...), condition=%wide.region_23.24_spmd, body=%wide.region_12.23_spmd.sunk | while | flops 579658816 | bytes 12476461 | solution.py:131
  410.9 1.5 bitcast_dynamic-update-slice_fusion.7
  414.3 2.1 multiply_reduce_fusion.11
  416.6 1.3 fusion.136
  426.9 1.5 bitcast_dynamic-update-slice_fusion.7
  430.2 2.1 multiply_reduce_fusion.11
  432.5 1.3 fusion.136
  439.9 140.0 %psum.23 = f32[1,16]{1,0:T(1,128)} all-reduce(f32[1,16]{1,0:T(1,128)S(1)} %bitcast.251), channel_id=1, replica_groups=mesh['dp'=8,'ctx'=64,'tensor'=2] {'ctx'}, use_global_device_ids=true, to_apply=%region_27.28 | all-reduce | flops 16 | bytes 128 | tf_op jit(solution)/shard_map/psum | solution.py:201
  579.9 1.5 copy.53
  583.1 1.5 copy.143
  584.6 1.5 copy.144
  (268 shorter events, 119.9 us)
Async XLA Ops:
  7.2 320.8 %all-gather.4.cloned.1.call-start = ((), (), s32[]{:S(2)}) async-start(), calls=%async_computation | async-start | bytes 34078720 | tf_op jit(solution)/shard_map/all_gather | solution.py:14
  18.6 0.8 copy-start
  19.5 563.6 %all-reduce.4.cloned.1.call-start = ((), (), s32[]{:S(2)}) async-start(), calls=%async_computation.1 | async-start | bytes 262144 | tf_op jit(solution)/shard_map/psum | solution.py:200
  439.2 0.6 copy-start.1
  439.2 0.6 copy-start.2
Sparse Core Ops, SparseCore 0:
  19.6 308.2 all-gather.3
  440.0 40.2 all-reduce.3
where the time goes:
time: 598 us; the launch traced here: 593 us
  blocking collectives  299 us (50%)
  waiting for transfers between devices  130 us (22%)
  other arithmetic  95.6 us (16%)
  local copies, waits for them, and re-layouts  25.4 us (4%)
  matrix products  24.9 us (4%)
  between operations  15.5 us (3%)
    unnamed x1, blocking collectives  159 us
    psum x1, blocking collectives, per_device(): drate_sum = lax.psum(drate_local, 'ctx')  140 us
    all_gather x1, waiting for transfers between devices, carried_in(): everything = jax.tree.map(lambda part: lax.all_gather(part, axis), x)  130 us
    select_n x64, other arithmetic, step(): return jax.tree.map(lambda a, b: jnp.where(reached, a, b), new, before)  75.2 us
  transfers between devices with their start and end apart: 2, of which 1 were waited for; matrix products, arithmetic and copies ran while one was open for 4% of the time, Pallas kernels for 0%

commit v1 on v0

v1 whole, which is shorter than its diff:
```python
import jax
import jax.numpy as jnp
from jax import lax
from jax.experimental import pallas as pl
from jax.experimental.pallas import tpu as pltpu
from jax.sharding import Mesh, PartitionSpec as P

F32 = jnp.float32
BF16 = jnp.bfloat16
LANES = 128
HIGHEST = lax.Precision.HIGHEST
INTERPRET = False


def mm(a, b):
    return lax.dot_general(a, b, (((1,), (0,)), ((), ())), preferred_element_type=F32)


def mmt(a, b):
    return lax.dot_general(a, b, (((1,), (1,)), ((), ())), preferred_element_type=F32)


def mm_exact(a, b):
    return lax.dot_general(
        a, b, (((1,), (0,)), ((), ())), precision=HIGHEST, preferred_element_type=F32
    )


def mmt_exact(a, b):
    return lax.dot_general(
        a, b, (((1,), (1,)), ((), ())), precision=HIGHEST, preferred_element_type=F32
    )


def split2(a):
    hi = a.astype(BF16)
    return hi, (a - hi.astype(F32)).astype(BF16)


def split3(a):
    hi = a.astype(BF16)
    rest = a - hi.astype(F32)
    mid = rest.astype(BF16)
    return hi, mid, (rest - mid.astype(F32)).astype(BF16)


def iota(shape, dim):
    return lax.broadcasted_iota(jnp.int32, shape, dim)


def head_rows(rows, width, head_dim):
    return (iota((rows, width), 0) == iota((rows, width), 1) // head_dim).astype(BF16)


def expand(per_head, width, head_dim):
    hot = head_rows(LANES, width, head_dim)
    hi, mid, low = split3(per_head)
    return mm(hi, hot) + mm(mid, hot) + mm(low, hot)


def decays(dt, rates, start):
    heads, tok = dt.shape
    log_step = -dt * rates
    log_step = jnp.concatenate([log_step, jnp.zeros((LANES - heads, tok), F32)], axis=0)
    lower = (iota((tok, tok), 0) >= iota((tok, tok), 1)).astype(F32)
    log_cum = mmt_exact(lower, log_step)
    starts = jnp.broadcast_to(start.astype(F32), (tok, tok))
    docs_down = mmt(lower.astype(BF16), starts.astype(BF16))
    return log_cum, docs_down, starts


def acc_kernel(dy_ref, dt_ref, c_ref, st_ref, rates_ref, out_ref):
    tok, width = dy_ref.shape
    heads = dt_ref.shape[0]
    slices, rows, _ = out_ref.shape
    log_cum, docs, _ = decays(dt_ref[...], rates_ref[...], st_ref[...])
    entry = jnp.where(docs == 0.0, jnp.exp(log_cum), 0.0)
    wide = expand(entry, width, width // heads)
    hi, low = split2(dy_ref[...].astype(F32) * wide)
    eye = (iota((LANES, LANES), 0) == iota((LANES, LANES), 1)).astype(BF16)
    c_t = mmt(eye, c_ref[...]).astype(BF16)
    acc = mm(c_t, hi) + mm(c_t, low)
    last = jnp.broadcast_to(entry[tok - 1 : tok, :], (rows, LANES))
    for i in range(slices):
        out_ref[i, :, :width] = acc[i * rows : (i + 1) * rows, :]
        out_ref[i, :, width:] = last


def local_kernel(
    x_ref,
    dy_ref,
    dt_ref,
    b_ref,
    c_ref,
    h_ref,
    st_ref,
    rates_ref,
    a1_ref,
    a2_ref,
    tx_hi_ref,
    tx_low_ref,
    ht_ref,
    gb_ref,
    gc_ref,
    z_ref,
    q_ref,
    dec_ref,
):
    tok, width = dy_ref.shape
    heads = dt_ref.shape[0]
    head_dim = width // heads
    dt = dt_ref[...]
    log_cum, docs, starts = decays(dt, rates_ref[...], st_ref[...])
    row = iota((tok, tok), 0)
    col = iota((tok, tok), 1)
    upper = (row <= col).astype(BF16)
    docs_across = mm(starts.astype(BF16), upper)
    same = docs == docs_across
    mask = jnp.where(same & (row >= col), 1.0, 0.0)
    mask_t = jnp.where(same & (row <= col), 1.0, 0.0)
    eye = (row == col).astype(F32)
    dt_pad = jnp.concatenate([dt, jnp.zeros((LANES - heads, tok), F32)], axis=0)
    dt_down = mmt_exact(eye, dt_pad)
    growth = jnp.exp(log_cum)
    e_wide = expand(growth, width, head_dim)
    s_wide = expand(jnp.exp(-log_cum) * dt_down, width, head_dim)
    first = jnp.where(docs == 0.0, 1.0, 0.0)
    tail = jnp.where(docs == docs[tok - 1 : tok, :], 1.0, 0.0)
    times = width // LANES
    first_wide = jnp.concatenate([first] * times, axis=1)
    tail_wide = jnp.concatenate([tail] * times, axis=1)
    to_end = s_wide * e_wide[tok - 1 : tok, :] * tail_wide
    x = x_ref[...].astype(F32)
    ey = dy_ref[...].astype(F32) * e_wide
    xs = x * s_wide
    a2_ref[...] = to_end
    tx_hi, tx_low = split2(x * to_end)
    tx_hi_ref[...] = tx_hi
    tx_low_ref[...] = tx_low
    ey_hi, ey_low = split2(ey)
    xs_hi, xs_low = split2(xs)
    h = h_ref[...]
    h_hi, h_low = split2(h)
    ht_ref[...] = h.T
    b = b_ref[...]
    c = c_ref[...]

    weight = mask * (mmt(ey_hi, xs_hi) + mmt(ey_hi, xs_low) + mmt(ey_low, xs_hi))
    w_hi, w_low = split2(weight)
    wt_hi, wt_low = split2(weight.T)
    zero = jnp.zeros((), BF16)
    keep = first_wide > 0.5
    f_hi = jnp.where(keep, ey_hi, zero)
    f_low = jnp.where(keep, ey_low, zero)
    gc_ref[...] = mm(w_hi, b) + mm(w_low, b) + mm(f_hi, h_hi) + mm(f_hi, h_low) + mm(f_low, h_hi)
    gb_ref[...] = mm(wt_hi, c) + mm(wt_low, c)

    g_hi, g_low = split2(mask * mmt(c, b))
    gt_hi, gt_low = split2(mask_t * mmt(b, c))
    a1_ref[...] = s_wide * (mm(gt_hi, ey_hi) + mm(gt_hi, ey_low) + mm(gt_low, ey_hi))
    from_h = first_wide * (mmt(c, h_hi) + mmt(c, h_low))
    y = mm(g_hi, xs_hi) + mm(g_hi, xs_low) + mm(g_low, xs_hi) + from_h
    hot = head_rows(heads, width, head_dim)
    z_hi, z_low = split2(ey * y)
    z_ref[...] = mmt(hot, z_hi) + mmt(hot, z_low)
    q_hi, q_low = split2(ey * from_h)
    q = jnp.sum(mmt(hot, q_hi) + mmt(hot, q_low), axis=1, keepdims=True)
    q_ref[...] = jnp.broadcast_to(q, (heads, tok))
    total = jnp.sum(dt, axis=1, keepdims=True)
    none = jnp.max(starts[:1, :], axis=1, keepdims=True) < 0.5
    dec = jnp.where(none, jnp.exp(-rates_ref[...] * total), 0.0)
    dec_ref[...] = jnp.broadcast_to(dec, (heads, tok))


def total_kernel(got_ref, out_ref, *, width, head_dim):
    members, rows, _ = got_ref.shape
    dec = jnp.concatenate([got_ref[k, :1, width:] for k in range(members)], axis=0)
    wide = expand(dec, width, head_dim)
    carry = got_ref[members - 1, :, :width]
    whole = dec[members - 1 : members, :]
    for k in range(members - 2, -1, -1):
        carry = got_ref[k, :, :width] + wide[k : k + 1, :] * carry
        whole = whole * dec[k : k + 1, :]
    for i in range(out_ref.shape[0]):
        out_ref[i, :, :width] = carry
        out_ref[i, :, width:] = jnp.broadcast_to(whole, (rows, LANES))


def carry_kernel(me_ref, got_ref, totals_ref, out_ref, *, width, head_dim):
    members, rows, _ = got_ref.shape
    groups = totals_ref.shape[0]
    me = me_ref[0]
    dec = jnp.concatenate([totals_ref[k, :1, width:] for k in range(groups)], axis=0)
    dec = jnp.concatenate([dec, jnp.zeros((8 - groups % 8, LANES), F32)], axis=0)
    wide = expand(dec, width, head_dim)
    carry = jnp.zeros((rows, width), F32)
    for k in range(groups - 1, 0, -1):
        new = totals_ref[k, :, :width] + wide[k : k + 1, :] * carry
        carry = jnp.where(k > me, new, carry)
    dec = jnp.concatenate([got_ref[k, :1, width:] for k in range(members)], axis=0)
    wide = expand(dec, width, head_dim)
    for k in range(members - 1, -1, -1):
        out_ref[k, :, :] = carry
        if k:
            carry = got_ref[k, :, :width] + wide[k : k + 1, :] * carry


def final_kernel(
    f_ref,
    x_ref,
    dt_ref,
    b_ref,
    rates_ref,
    a1_ref,
    a2_ref,
    tx_hi_ref,
    tx_low_ref,
    ht_ref,
    gb_ref,
    z_ref,
    q_ref,
    dec_ref,
    gx_ref,
    gdt_ref,
    gb_out_ref,
    dr_ref,
):
    tok, width = x_ref.shape
    heads = dt_ref.shape[0]
    f = jnp.concatenate([f_ref[k] for k in range(f_ref.shape[0])], axis=0)
    f_hi, f_low = split2(f)
    b = b_ref[...]
    gx = a1_ref[...] + a2_ref[...] * (mm(b, f_hi) + mm(b, f_low))
    gx_ref[...] = gx.astype(BF16)
    tx_hi = tx_hi_ref[...]
    gb_out_ref[...] = (
        gb_ref[...] + mmt(tx_hi, f_hi) + mmt(tx_hi, f_low) + mmt(tx_low_ref[...], f_hi)
    )
    hot = head_rows(heads, width, width // heads)
    s_hi, s_low = split2(x_ref[...].astype(F32) * gx)
    ds_s = mmt(hot, s_hi) + mmt(hot, s_low)
    p_hi, p_low = split2(f * ht_ref[...])
    f_h = jnp.sum(mmt(hot, p_hi) + mmt(hot, p_low), axis=1, keepdims=True)
    before = (iota((tok, tok), 0) < iota((tok, tok), 1)).astype(F32)
    r = mm_exact(ds_s - z_ref[...], before) + (q_ref[...] + dec_ref[...] * f_h)
    dt = dt_ref[...]
    gdt_ref[...] = ds_s / dt - rates_ref[...] * r
    dr = -jnp.sum(dt * r, axis=1, keepdims=True)
    dr_ref[...] = jnp.broadcast_to(dr, (heads, LANES))


def call(kernel, outs, *args, scalars=0):
    vmem = pl.BlockSpec(memory_space=pltpu.VMEM)
    smem = pl.BlockSpec(memory_space=pltpu.SMEM)
    return pl.pallas_call(
        kernel,
        out_shape=[jax.ShapeDtypeStruct(s, d) for s, d in outs],
        in_specs=[smem] * scalars + [vmem] * (len(args) - scalars),
        out_specs=[vmem] * len(outs),
        interpret=INTERPRET,
    )(*args)


def per_device(x_seq, dt_seq, b_seq, c_seq, dy_seq, saved_states, doc_starts, decay_rates):
    heads = decay_rates.shape[0]
    tok, width = x_seq.shape[1:]
    head_dim = width // heads
    n = b_seq.shape[2]
    groups = lax.axis_size("zo")
    near = lax.axis_size("zi") * lax.axis_size("cx")
    rows = n // near
    x, dt, b, c, dy = (a[0] for a in (x_seq, dt_seq, b_seq, c_seq, dy_seq))
    h = saved_states[0, 0]
    rates = decay_rates[:, None]
    (acc,) = call(acc_kernel, [((near, rows, width + LANES), F32)], dy, dt, c, doc_starts, rates)
    got = lax.all_to_all(acc, ("zi", "cx"), 0, 0)
    wide, small, square = (tok, width), (heads, tok), (tok, n)
    a1, a2, tx_hi, tx_low, ht, gb, gc, z, q, dec = call(
        local_kernel,
        [
            (wide, F32),
            (wide, F32),
            (wide, BF16),
            (wide, BF16),
            ((n, width), F32),
            (square, F32),
            (square, F32),
            (small, F32),
            (small, F32),
            (small, F32),
        ],
        *(x, dy, dt, b, c, h, doc_starts, rates),
    )
    swap = [(0, 1), (1, 0)]
    gc_sum = gc + lax.ppermute(gc, "tensor", swap)

    def totals(got_ref, out_ref):
        total_kernel(got_ref, out_ref, width=width, head_dim=head_dim)

    (total,) = call(totals, [((groups, rows, width + LANES), F32)], got)
    spread = lax.all_to_all(total, "zo", 0, 0)

    def carries(me_ref, got_ref, totals_ref, out_ref):
        carry_kernel(me_ref, got_ref, totals_ref, out_ref, width=width, head_dim=head_dim)

    me = lax.axis_index("zo").astype(jnp.int32).reshape(1)
    (carry,) = call(carries, [((near, rows, width), F32)], me, got, spread, scalars=1)
    incoming = lax.all_to_all(carry, ("zi", "cx"), 0, 0)
    gx, gdt, gb_all, dr = call(
        final_kernel,
        [(wide, BF16), (small, F32), (square, F32), ((heads, LANES), F32)],
        *(incoming, x, dt, b, rates, a1, a2, tx_hi, tx_low, ht, gb, z, q, dec),
    )
    gb_sum = gb_all + lax.ppermute(gb_all, "tensor", swap)
    ctx = groups * near
    dr_all = jnp.broadcast_to(dr[:, 0].reshape(1, 1, heads), (ctx, 1, heads))
    dr_sum = jnp.sum(lax.all_to_all(dr_all, ("zo", "zi", "cx"), 0, 0), axis=0)
    return gx[None], gdt[None], gb_sum[None], gc_sum[None], dr_sum


def solution(mesh):
    sizes = dict(mesh.shape)
    dp, ctx, tensor = sizes["dp"], sizes["ctx"], sizes["tensor"]
    inner = 4 if ctx % 64 == 0 else 2
    names = ("dp", "zo", "zi", "cx", "tensor")
    split = Mesh(mesh.devices.reshape(dp, ctx // inner**2, inner, inner, tensor), names)
    ctx_axes = ("zo", "zi", "cx")
    return jax.shard_map(
        per_device,
        mesh=split,
        in_specs=(
            P("dp", ctx_axes, "tensor"),
            P("dp", "tensor", ctx_axes),
            P("dp", ctx_axes, None),
            P("dp", ctx_axes, None),
            P("dp", ctx_axes, "tensor"),
            P("dp", ctx_axes, "tensor", None),
            P("dp", ctx_axes),
            P("tensor"),
        ),
        out_specs=(
            P("dp", ctx_axes, "tensor"),
            P("dp", "tensor", ctx_axes),
            P("dp", ctx_axes, None),
            P("dp", ctx_axes, None),
            P("dp", "tensor"),
        ),
        check_vma=False,
    )
```

time: 598 us -> 116 us (0.19)
  blocking collectives: 299 us -> 27.8 us
  waiting for transfers between devices: 130 us -> 34.1 us
  other arithmetic: 95.6 us -> 1.87 us
  starting transfers between devices: 0.08 us -> 30.9 us
  matrix products: 24.9 us -> 0 us
  local copies, waits for them, and re-layouts: 25.4 us -> 4.25 us
  Pallas kernels: 0 us -> 15.3 us
  between operations: 15.5 us -> 0.71 us
    unnamed x1 -> x0, blocking collectives: 159 us -> none
    psum x1 -> x0, blocking collectives: 140 us -> none  [per_device(): drate_sum = lax.psum(drate_local, 'ctx')]
    all_gather x1 -> x0, waiting for transfers between devices: 130 us -> none  [carried_in(): everything = jax.tree.map(lambda part: lax.all_gather(part, axis), x)]
    select_n x70 -> x0, other arithmetic: 75.5 us -> none  [the longest x64 75.2 us: step(): return jax.tree.map(lambda a, b: jnp.where(reached, a, b), new, before)]
    all_to_all x0 -> x3, waiting for transfers between devices: none -> 34.1 us  [the longest x1 15.4 us: per_device(): spread = lax.all_to_all(total, 'zo', 0, 0)]
    all_to_all x0 -> x1, blocking collectives: none -> 27.8 us  [per_device(): got = lax.all_to_all(acc, ('zi', 'cx'), 0, 0)]
    all_to_all x0 -> x3, starting transfers between devices: none -> 27.1 us  [the longest x1 16 us: per_device(): spread = lax.all_to_all(total, 'zo', 0, 0)]
    dot_general x32 -> x0, matrix products: 24.9 us -> none  [the longest x2 4.3 us: block_grads(): jnp.einsum('htp,hpn->htn', dy_blk, h_init, precision=HIGHEST_PREC)]
  transfers between devices with their start and end apart: 2 -> 5, of which waited for: 1 -> 3; matrix products, arithmetic and copies ran while one was open for 4% -> 2% of each run, Pallas kernels for 0% -> 7%
where the time goes in v1:
time: 116 us; the launch traced here: 115 us
  waiting for transfers between devices  34.1 us (29%)
  starting transfers between devices  30.9 us (27%)
  blocking collectives  27.8 us (24%)
  Pallas kernels  15.3 us (13%)
  local copies, waits for them, and re-layouts  4.25 us (4%)
  other arithmetic  1.87 us (2%)
    all_to_all x1, blocking collectives, per_device(): got = lax.all_to_all(acc, ('zi', 'cx'), 0, 0)  27.8 us
    all_to_all x1, starting transfers between devices, per_device(): spread = lax.all_to_all(total, 'zo', 0, 0)  16 us
    all_to_all x1, waiting for transfers between devices, per_device(): spread = lax.all_to_all(total, 'zo', 0, 0)  15.4 us
    pallas_call x5, Pallas kernels, call(): pl.pallas_call(kernel, out_shape=[jax.ShapeDtypeStruct(s, d) for s, d in...  15.3 us
    all_to_all x1, waiting for transfers between devices, per_device(): dr_sum = jnp.sum(lax.all_to_all(dr_all, ('zo', 'zi', 'cx'), 0, 0), axis=0)  12.2 us
    all_to_all x1, starting transfers between devices, per_device(): dr_sum = jnp.sum(lax.all_to_all(dr_all, ('zo', 'zi', 'cx'), 0, 0), axis=0)  7.01 us
    all_to_all x1, waiting for transfers between devices, per_device(): incoming = lax.all_to_all(carry, ('zi', 'cx'), 0, 0)  6.53 us
    all_to_all x1, starting transfers between devices, per_device(): incoming = lax.all_to_all(carry, ('zi', 'cx'), 0, 0)  4.07 us
  transfers between devices with their start and end apart: 5, of which 3 were waited for; matrix products, arithmetic and copies ran while one was open for 2% of the time, Pallas kernels for 7%

profile of v1, /device:TPU:56, one launch (start us, length us, event | category | flops | bytes accessed | tf_op | source)
XLA Modules:
  0.0 115.0 jit_solution(7443009582221044242)
XLA Ops:
  0.6 0.6 copy-done.4
  1.3 0.7 copy.22.rates_ref
  2.0 2.9 %shard_map.119 = f32[16,8,1152]{2,1,0:T(8,128)} custom-call(bf16[128,1024]{1,0:T(8,128)(2,1)} %bitcast.15, f32[16,128]{1,0:T(8,128)} %bitcast.24, bf16[128,128]{1,0:T(8,128)(2,1)} %bitcast.22, s32[1,128]{1,0:T(1,128)} %st_ref.3, f32[16,1]{1,0:T(8,128)} %copy.22.rates_ref), custom_call_target="tpu_custom_call" | custom-call | tf_op jit(solution)/shard_map/pallas_call | solution.py:255
  4.9 27.8 %all_to_all.20.got_ref = f32[16,8,1152]{2,1,0:T(8,128)} all-to-all(f32[16,8,1152]{2,1,0:T(8,128)} %shard_map.119), channel_id=1, replica_groups=mesh['dp'=8,'zo'=4,'zi'=4,'cx'=4,'tensor'=2] {'zi','cx'}, dimensions={0} | all-to-all | bytes 1179648 | tf_op jit(solution)/shard_map/all_to_all | solution.py:276
  32.7 2.0 %shard_map.120 = f32[4,8,1152]{2,1,0:T(8,128)} custom-call(f32[16,8,1152]{2,1,0:T(8,128)} %all_to_all.20.got_ref), custom_call_target="tpu_custom_call" | custom-call | tf_op jit(solution)/shard_map/pallas_call | solution.py:255
  34.7 16.0 %all-to-all-start.1 = ((f32[4,8,1152]{2,1,0:T(8,128)}), f32[4,8,1152]{2,1,0:T(8,128)S(1)}, u32[]{:S(2)}, u32[]{:S(2)}) async-start(f32[4,8,1152]{2,1,0:T(8,128)} %shard_map.120), calls=%async_computation.1 | async-start | bytes 294912 | tf_op jit(solution)/shard_map/all_to_all | solution.py:301
  50.7 15.4 %all-to-all-done.1.totals_ref = f32[4,8,1152]{2,1,0:T(8,128)S(1)} async-done(((f32[4,8,1152]{2,1,0:T(8,128)}), f32[4,8,1152]{2,1,0:T(8,128)S(1)}, u32[]{:S(2)}, u32[]{:S(2)}) %all-to-all-start.1) | async-done | bytes 147488 | tf_op jit(solution)/shard_map/all_to_all | solution.py:301
  66.1 0.7 copy-done.1
  66.7 2.2 %shard_map.121 = f32[16,8,1024]{2,1,0:T(8,128)} custom-call(s32[1]{0:T(128)} %bitcast.me_ref, f32[16,8,1152]{2,1,0:T(8,128)} %all_to_all.20.got_ref, f32[4,8,1152]{2,1,0:T(8,128)} %copy-done.1), custom_call_target="tpu_custom_call" | custom-call | tf_op jit(solution)/shard_map/pallas_call | solution.py:255
  68.9 4.1 %all-to-all-start.2 = ((f32[16,8,1024]{2,1,0:T(8,128)}), f32[16,8,1024]{2,1,0:T(8,128)S(1)}, u32[]{:S(2)}, u32[]{:S(2)}) async-start(f32[16,8,1024]{2,1,0:T(8,128)} %shard_map.121), calls=%async_computation.2 | async-start | bytes 1048576 | tf_op jit(solution)/shard_map/all_to_all | solution.py:308
  73.0 4.6 %shard_map.122 = (f32[128,1024]{1,0:T(8,128)}, f32[128,1024]{1,0:T(8,128)}, bf16[128,1024]{1,0:T(8,128)(2,1)}, bf16[128,1024]{1,0:T(8,128)(2,1)}, f32[128,1024]{...) custom-call(bf16[128,1024]{1,0:T(8,128)(2,1)} %bitcast.17, ...), custom_call_target="tpu_custom_call" | custom-call | tf_op jit(solution)/shard_map/pallas_call | solution.py:255
  77.6 1.9 %collective-permute-start.1 = (f32[128,128]{1,0:T(8,128)}, f32[128,128]{1,0:T(8,128)S(1)}, u32[]{:S(2)}, u32[]{:S(2)}) collective-permute-start(f32[128,128]{1,0:T(8,128)} %get-tuple-element.31), channel_id=1, source_target_pairs={{0,1},{1,0},{2,3},{3,2},{4,5},{5,4},{6,7},{7,6},{8,9},{9,8},{10,11... | collective-permute-start | bytes 196616 | tf_op jit(solution)/shard_map/ppermute | solution.py:295
  79.5 6.5 %all-to-all-done.2.f_ref = f32[16,8,1024]{2,1,0:T(8,128)S(1)} async-done(((f32[16,8,1024]{2,1,0:T(8,128)}), f32[16,8,1024]{2,1,0:T(8,128)S(1)}, u32[]{:S(2)}, u32[]{:S(2)}) %all-to-all-start.2) | async-done | bytes 524320 | tf_op jit(solution)/shard_map/all_to_all | solution.py:308
  86.1 0.8 copy-done
  86.9 3.6 %shard_map.123 = (bf16[128,1024]{1,0:T(8,128)(2,1)}, f32[16,128]{1,0:T(8,128)}, f32[128,128]{1,0:T(8,128)}, f32[16,128]{1,0:T(8,128)}) custom-call(f32[16,8,1024]{2,1,0:T(8,128)} %copy-done, bf16[128,1024]{1,0:T(8,128)(2,1)} %bitcast.18, f32[16,128]{1,0:T(8,128)} %bitcast.26, bf16[128,128]{1,0:T(8,128)(2,1)} %bitcast.21, f32[16,1]{1,0:T(8,128)} %copy.22.rates_ref, ...), custom_call_target="tpu_custom_call" | custom-call | tf_op jit(solution)/shard_map/pallas_call | solution.py:255
  90.5 0.8 slice_reduce_fusion
  91.3 0.6 broadcast_in_dim.28
  91.9 7.0 %all-to-all-start.3 = ((f32[64,1,16]{2,1,0:T(1,128)}), f32[64,1,16]{2,1,0:T(1,128)S(1)}, u32[]{:S(2)}, u32[]{:S(2)}) async-start(f32[64,1,16]{2,1,0:T(1,128)} %broadcast_in_dim.28), calls=%async_computation.3 | async-start | bytes 65536 | tf_op jit(solution)/shard_map/all_to_all | solution.py:317
  99.0 1.9 %collective-permute-start = (f32[128,128]{1,0:T(8,128)S(1)}, f32[128,128]{1,0:T(8,128)S(1)}, u32[]{:S(2)}, u32[]{:S(2)}) collective-permute-start(f32[128,128]{1,0:T(8,128)S(1)} %copy-done.2), channel_id=1, source_target_pairs={{0,1},{1,0},{2,3},{3,2},{4,5},{5,4},{6,7},{7,6},{8,9},{9,8},{10,11... | collective-permute-start | bytes 196616 | tf_op jit(solution)/shard_map/ppermute | solution.py:314
  100.9 0.0 collective-permute-done.1
  100.9 0.6 add_bitcast_fusion
  101.5 12.2 %all-to-all-done.3 = f32[64,1,16]{2,1,0:T(1,128)S(1)} async-done(((f32[64,1,16]{2,1,0:T(1,128)}), f32[64,1,16]{2,1,0:T(1,128)S(1)}, u32[]{:S(2)}, u32[]{:S(2)}) %all-to-all-start.3) | async-done | bytes 4128 | tf_op jit(solution)/shard_map/all_to_all | solution.py:317
  113.8 0.6 reduce_sum.11
  114.3 0.6 add_bitcast_fusion.1
  (8 shorter events, 0.0 us)
Async XLA Ops:
  0.6 0.7 copy-start.4
  34.7 31.4 %all-to-all-start.1 = ((f32[4,8,1152]{2,1,0:T(8,128)}), f32[4,8,1152]{2,1,0:T(8,128)S(1)}, u32[]{:S(2)}, u32[]{:S(2)}) async-start(f32[4,8,1152]{2,1,0:T(8,128)} %shard_map.120), calls=%async_computation.1 | async-start | bytes 294912 | tf_op jit(solution)/shard_map/all_to_all | solution.py:301
  66.1 0.7 copy-start.1
  68.9 17.2 %all-to-all-start.2 = ((f32[16,8,1024]{2,1,0:T(8,128)}), f32[16,8,1024]{2,1,0:T(8,128)S(1)}, u32[]{:S(2)}, u32[]{:S(2)}) async-start(f32[16,8,1024]{2,1,0:T(8,128)} %shard_map.121), calls=%async_computation.2 | async-start | bytes 1048576 | tf_op jit(solution)/shard_map/all_to_all | solution.py:308
  77.6 23.3 %collective-permute-start.1 = (f32[128,128]{1,0:T(8,128)}, f32[128,128]{1,0:T(8,128)S(1)}, u32[]{:S(2)}, u32[]{:S(2)}) collective-permute-start(f32[128,128]{1,0:T(8,128)} %get-tuple-element.31), channel_id=1, source_target_pairs={{0,1},{1,0},{2,3},{3,2},{4,5},{5,4},{6,7},{7,6},{8,9},{9,8},{10,11... | collective-permute-start | bytes 196616 | tf_op jit(solution)/shard_map/ppermute | solution.py:295
  86.1 0.8 copy-start
  86.9 14.0 %copy-start.3 = (f32[128,128]{1,0:T(8,128)S(1)}, f32[128,128]{1,0:T(8,128)}, u32[]{:S(2)}) copy-start(f32[128,128]{1,0:T(8,128)} %get-tuple-element.31) | copy-start | bytes 196612
  90.4 8.5 %copy-start.2 = (f32[128,128]{1,0:T(8,128)S(1)}, f32[128,128]{1,0:T(8,128)}, u32[]{:S(2)}) copy-start(f32[128,128]{1,0:T(8,128)} %get-tuple-element.30) | copy-start | bytes 196612
  91.9 21.8 %all-to-all-start.3 = ((f32[64,1,16]{2,1,0:T(1,128)}), f32[64,1,16]{2,1,0:T(1,128)S(1)}, u32[]{:S(2)}, u32[]{:S(2)}) async-start(f32[64,1,16]{2,1,0:T(1,128)} %broadcast_in_dim.28), calls=%async_computation.3 | async-start | bytes 65536 | tf_op jit(solution)/shard_map/all_to_all | solution.py:317
  99.0 15.4 %collective-permute-start = (f32[128,128]{1,0:T(8,128)S(1)}, f32[128,128]{1,0:T(8,128)S(1)}, u32[]{:S(2)}, u32[]{:S(2)}) collective-permute-start(f32[128,128]{1,0:T(8,128)S(1)} %copy-done.2), channel_id=1, source_target_pairs={{0,1},{1,0},{2,3},{3,2},{4,5},{5,4},{6,7},{7,6},{8,9},{9,8},{10,11... | collective-permute-start | bytes 196616 | tf_op jit(solution)/shard_map/ppermute | solution.py:314

commit v2 on v1

--- a/solution.py
+++ b/solution.py
@@ -60,10 +60,10 @@
 
 def decays(dt, rates, start):
     heads, tok = dt.shape
-    log_step = -dt * rates
-    log_step = jnp.concatenate([log_step, jnp.zeros((LANES - heads, tok), F32)], axis=0)
+    dt = jnp.concatenate([dt, jnp.zeros((LANES - heads, tok), F32)], axis=0)
     lower = (iota((tok, tok), 0) >= iota((tok, tok), 1)).astype(F32)
-    log_cum = mmt_exact(lower, log_step)
+    rates = jnp.concatenate([rates, jnp.zeros((1, LANES - heads), F32)], axis=1)
+    log_cum = -rates * mmt_exact(lower, dt)
     starts = jnp.broadcast_to(start.astype(F32), (tok, tok))
     docs_down = mmt(lower.astype(BF16), starts.astype(BF16))
     return log_cum, docs_down, starts
@@ -105,6 +105,9 @@
     z_ref,
     q_ref,
     dec_ref,
+    lam_ref,
+    mt_ref,
+    dr_ref,
 ):
     tok, width = dy_ref.shape
     heads = dt_ref.shape[0]
@@ -141,7 +144,8 @@
     xs_hi, xs_low = split2(xs)
     h = h_ref[...]
     h_hi, h_low = split2(h)
-    ht_ref[...] = h.T
+    ht = h.T
+    ht_ref[...] = ht
     b = b_ref[...]
     c = c_ref[...]
 
@@ -157,19 +161,49 @@
 
     g_hi, g_low = split2(mask * mmt(c, b))
     gt_hi, gt_low = split2(mask_t * mmt(b, c))
-    a1_ref[...] = s_wide * (mm(gt_hi, ey_hi) + mm(gt_hi, ey_low) + mm(gt_low, ey_hi))
+    a1 = s_wide * (mm(gt_hi, ey_hi) + mm(gt_hi, ey_low) + mm(gt_low, ey_hi))
+    a1_ref[...] = a1
     from_h = first_wide * (mmt(c, h_hi) + mmt(c, h_low))
     y = mm(g_hi, xs_hi) + mm(g_hi, xs_low) + mm(g_low, xs_hi) + from_h
     hot = head_rows(heads, width, head_dim)
     z_hi, z_low = split2(ey * y)
-    z_ref[...] = mmt(hot, z_hi) + mmt(hot, z_low)
+    z = mmt(hot, z_hi) + mmt(hot, z_low)
+    z_ref[...] = z
     q_hi, q_low = split2(ey * from_h)
     q = jnp.sum(mmt(hot, q_hi) + mmt(hot, q_low), axis=1, keepdims=True)
     q_ref[...] = jnp.broadcast_to(q, (heads, tok))
+    rates = jnp.concatenate([rates_ref[...], jnp.zeros((1, LANES - heads), F32)], axis=1)
+    diag = iota((heads, LANES), 0) == iota((heads, LANES), 1)
+    lam = mmt_exact(jnp.where(diag, rates, 0.0), jnp.ones((tok, LANES), F32))
+    lam_ref[...] = lam
     total = jnp.sum(dt, axis=1, keepdims=True)
     none = jnp.max(starts[:1, :], axis=1, keepdims=True) < 0.5
-    dec = jnp.where(none, jnp.exp(-rates_ref[...] * total), 0.0)
-    dec_ref[...] = jnp.broadcast_to(dec, (heads, tok))
+    dec_ref[...] = jnp.where(none, jnp.exp(-lam * total), 0.0)
+
+    s_hi, s_low = split2(x * a1)
+    before = (row < col).astype(F32)
+    r = mm_exact(mmt(hot, s_hi) + mmt(hot, s_low) - z, before) + q
+    local = -jnp.sum(dt * r, axis=1, keepdims=True)
+    dr_ref[...] = jnp.sum(jnp.where(diag, local, 0.0), axis=0, keepdims=True)
+    later_wide = expand(mmt_exact(before, dt_pad), width, head_dim)
+    b_t = mmt(eye.astype(BF16), b).astype(BF16)
+    m_hi, m_low = split2(x * to_end * later_wide)
+    all_dt = jnp.sum(dt_down, axis=0, keepdims=True)
+    last = jnp.where(docs[tok - 1 :, :] == 0.0, growth[tok - 1 :, :] * all_dt, 0.0)
+    mt_ref[...] = mm(b_t, m_hi) + mm(b_t, m_low) + ht * expand(last, width, head_dim)
+
+
+def rates_kernel(f_ref, mt_ref, dr_ref, out_ref, *, head_dim):
+    n, width = mt_ref.shape
+    ctx = out_ref.shape[0]
+    rows = f_ref.shape[1]
+    part = f_ref[0] * mt_ref[:rows, :]
+    for k in range(1, n // rows):
+        part = part + f_ref[k] * mt_ref[k * rows : (k + 1) * rows, :]
+    hot = head_rows(LANES, width, head_dim)
+    each = mmt_exact(part, hot.astype(F32))
+    out = dr_ref[...] - jnp.sum(each, axis=0, keepdims=True)
+    out_ref[...] = jnp.broadcast_to(out.reshape(1, 1, LANES), (ctx, 1, LANES))
 
 
 def total_kernel(got_ref, out_ref, *, width, head_dim):
@@ -210,7 +244,6 @@
     x_ref,
     dt_ref,
     b_ref,
-    rates_ref,
     a1_ref,
     a2_ref,
     tx_hi_ref,
@@ -220,11 +253,13 @@
     z_ref,
     q_ref,
     dec_ref,
+    lam_ref,
+    after_ref,
     gx_ref,
     gdt_ref,
     gb_out_ref,
-    dr_ref,
 ):
+    del after_ref
     tok, width = x_ref.shape
     heads = dt_ref.shape[0]
     f = jnp.concatenate([f_ref[k] for k in range(f_ref.shape[0])], axis=0)
@@ -243,20 +278,29 @@
     f_h = jnp.sum(mmt(hot, p_hi) + mmt(hot, p_low), axis=1, keepdims=True)
     before = (iota((tok, tok), 0) < iota((tok, tok), 1)).astype(F32)
     r = mm_exact(ds_s - z_ref[...], before) + (q_ref[...] + dec_ref[...] * f_h)
-    dt = dt_ref[...]
-    gdt_ref[...] = ds_s / dt - rates_ref[...] * r
-    dr = -jnp.sum(dt * r, axis=1, keepdims=True)
-    dr_ref[...] = jnp.broadcast_to(dr, (heads, LANES))
-
-
-def call(kernel, outs, *args, scalars=0):
+    gdt_ref[...] = ds_s / dt_ref[...] - lam_ref[...] * r
+
+
+def call(kernel, outs, *args, scalars=0, near=(), far=(), unread=0, mib=8):
     vmem = pl.BlockSpec(memory_space=pltpu.VMEM)
     smem = pl.BlockSpec(memory_space=pltpu.SMEM)
+    if INTERPRET:
+        shapes = [jax.ShapeDtypeStruct(s, d) for s, d, *_ in outs]
+    else:
+        shapes = [(pltpu.HBM if off else pltpu.VMEM)(s, d) for s, d, *off in outs]
+        place = {**dict.fromkeys(far, pltpu.HBM), **dict.fromkeys(near, pltpu.VMEM)}
+        args = [
+            pltpu.with_memory_space_constraint(a, place[i]) if i in place else a
+            for i, a in enumerate(args)
+        ]
     return pl.pallas_call(
         kernel,
-        out_shape=[jax.ShapeDtypeStruct(s, d) for s, d in outs],
-        in_specs=[smem] * scalars + [vmem] * (len(args) - scalars),
+        out_shape=shapes,
+        in_specs=[smem] * scalars
+        + [vmem] * (len(args) - scalars - unread)
+        + [pl.BlockSpec(memory_space=pl.ANY)] * unread,
         out_specs=[vmem] * len(outs),
+        compiler_params=pltpu.CompilerParams(vmem_limit_bytes=mib << 20),
         interpret=INTERPRET,
     )(*args)
 
@@ -268,53 +312,71 @@
     n = b_seq.shape[2]
     groups = lax.axis_size("zo")
     near = lax.axis_size("zi") * lax.axis_size("cx")
+    ctx = groups * near
     rows = n // near
     x, dt, b, c, dy = (a[0] for a in (x_seq, dt_seq, b_seq, c_seq, dy_seq))
     h = saved_states[0, 0]
-    rates = decay_rates[:, None]
+    rates = decay_rates[None]
     (acc,) = call(acc_kernel, [((near, rows, width + LANES), F32)], dy, dt, c, doc_starts, rates)
     got = lax.all_to_all(acc, ("zi", "cx"), 0, 0)
-    wide, small, square = (tok, width), (heads, tok), (tok, n)
-    a1, a2, tx_hi, tx_low, ht, gb, gc, z, q, dec = call(
+    wide, small, square, state = (tok, width), (heads, tok), (tok, n), (n, width)
+    local = call(
         local_kernel,
         [
-            (wide, F32),
-            (wide, F32),
-            (wide, BF16),
-            (wide, BF16),
-            ((n, width), F32),
+            (wide, F32, True),
+            (wide, F32, True),
+            (wide, BF16, True),
+            (wide, BF16, True),
+            (state, F32, True),
+            (square, F32, True),
             (square, F32),
-            (square, F32),
-            (small, F32),
-            (small, F32),
-            (small, F32),
+            (small, F32, True),
+            (small, F32, True),
+            (small, F32, True),
+            (small, F32, True),
+            (state, F32),
+            ((1, LANES), F32),
         ],
         *(x, dy, dt, b, c, h, doc_starts, rates),
-    )
+        mib=24,
+    )
+    a1, a2, tx_hi, tx_low, ht, gb, gc, z, q, dec, lam, mt, dr = local
     swap = [(0, 1), (1, 0)]
     gc_sum = gc + lax.ppermute(gc, "tensor", swap)
 
     def totals(got_ref, out_ref):
         total_kernel(got_ref, out_ref, width=width, head_dim=head_dim)
 
-    (total,) = call(totals, [((groups, rows, width + LANES), F32)], got)
+    (total,) = call(totals, [((groups, rows, width + LANES), F32)], got, near=(0,))
     spread = lax.all_to_all(total, "zo", 0, 0)
 
     def carries(me_ref, got_ref, totals_ref, out_ref):
         carry_kernel(me_ref, got_ref, totals_ref, out_ref, width=width, head_dim=head_dim)
 
     me = lax.axis_index("zo").astype(jnp.int32).reshape(1)
-    (carry,) = call(carries, [((near, rows, width), F32)], me, got, spread, scalars=1)
+    (carry,) = call(
+        carries, [((near, rows, width), F32)], me, got, spread, scalars=1, near=(1, 2)
+    )
     incoming = lax.all_to_all(carry, ("zi", "cx"), 0, 0)
-    gx, gdt, gb_all, dr = call(
+
+    def rates_sum(f_ref, mt_ref, dr_ref, out_ref):
+        rates_kernel(f_ref, mt_ref, dr_ref, out_ref, head_dim=head_dim)
+
+    (dr_all,) = call(
+        rates_sum, [((ctx, 1, LANES), F32)], incoming, mt, dr, near=(0, 1, 2)
+    )
+    dr_parts = lax.all_to_all(dr_all, ("zo", "zi", "cx"), 0, 0)
+    dr_sum = jnp.sum(dr_parts, axis=0)[:, :heads]
+    gx, gdt, gb_all = call(
         final_kernel,
-        [(wide, BF16), (small, F32), (square, F32), ((heads, LANES), F32)],
-        *(incoming, x, dt, b, rates, a1, a2, tx_hi, tx_low, ht, gb, z, q, dec),
+        [(wide, BF16, True), (small, F32, True), (square, F32)],
+        *(incoming, x, dt, b, a1, a2, tx_hi, tx_low, ht, gb, z, q, dec, lam, dr_all),
+        near=(0,),
+        far=range(4, 14),
+        unread=1,
+        mib=16,
     )
     gb_sum = gb_all + lax.ppermute(gb_all, "tensor", swap)
-    ctx = groups * near
-    dr_all = jnp.broadcast_to(dr[:, 0].reshape(1, 1, heads), (ctx, 1, heads))
-    dr_sum = jnp.sum(lax.all_to_all(dr_all, ("zo", "zi", "cx"), 0, 0), axis=0)
     return gx[None], gdt[None], gb_sum[None], gc_sum[None], dr_sum
 
 

time: 116 us -> 113 us (0.974)
  Pallas kernels: 15.3 us -> 11.9 us
  waiting for transfers between devices: 34.1 us -> 36 us
  local copies, waits for them, and re-layouts: 4.25 us -> 3.08 us
    pallas_call x5 -> x6, Pallas kernels: 15.3 us -> 11.9 us  [call(): pl.pallas_call(kernel, out_shape=shapes, in_specs=[smem] * scalars + [vme...]
    all_to_all x1, waiting for transfers between devices: 12.2 us -> 14 us  [per_device(): dr_parts = lax.all_to_all(dr_all, ('zo', 'zi', 'cx'), 0, 0)]
    broadcast_in_dim x2 -> x0, local copies, waits for them, and re-layouts: 1.31 us -> none  [the longest x1 0.68 us: per_device(): rates = decay_rates[:, None]]
    unnamed x10 -> x22, local copies, waits for them, and re-layouts: 2.1 us -> 3.08 us
  transfers between devices with their start and end apart: 5 -> 5, of which waited for: 3 -> 3; matrix products, arithmetic and copies ran while one was open for 2% -> 1% of each run, Pallas kernels for 7% -> 8%
where the time goes in v2:
time: 113 us; the launch traced here: 112 us
  waiting for transfers between devices  36 us (32%)
  starting transfers between devices  31.1 us (28%)
  blocking collectives  27.5 us (24%)
  Pallas kernels  11.9 us (11%)
  local copies, waits for them, and re-layouts  3.08 us (3%)
  other arithmetic  1.87 us (2%)
    all_to_all x1, blocking collectives, per_device(): got = lax.all_to_all(acc, ('zi', 'cx'), 0, 0)  27.5 us
    all_to_all x1, starting transfers between devices, per_device(): spread = lax.all_to_all(total, 'zo', 0, 0)  16 us
    all_to_all x1, waiting for transfers between devices, per_device(): spread = lax.all_to_all(total, 'zo', 0, 0)  15.4 us
    all_to_all x1, waiting for transfers between devices, per_device(): dr_parts = lax.all_to_all(dr_all, ('zo', 'zi', 'cx'), 0, 0)  14 us
    pallas_call x6, Pallas kernels, call(): pl.pallas_call(kernel, out_shape=shapes, in_specs=[smem] * scalars + [vme...  11.9 us
    all_to_all x1, starting transfers between devices, per_device(): dr_parts = lax.all_to_all(dr_all, ('zo', 'zi', 'cx'), 0, 0)  7.01 us
    all_to_all x1, waiting for transfers between devices, per_device(): incoming = lax.all_to_all(carry, ('zi', 'cx'), 0, 0)  6.6 us
    all_to_all x1, starting transfers between devices, per_device(): incoming = lax.all_to_all(carry, ('zi', 'cx'), 0, 0)  4.2 us
  transfers between devices with their start and end apart: 5, of which 3 were waited for; matrix products, arithmetic and copies ran while one was open for 1% of the time, Pallas kernels for 8%

profile of v2, /device:TPU:56, one launch (start us, length us, event | category | flops | bytes accessed | tf_op | source)
XLA Modules:
  0.0 112.2 jit_solution(8321100441122209531)
XLA Ops:
  0.7 0.6 copy-done.9
  1.3 0.0 copy-done.10
  1.3 0.9 copy-done.1
  2.3 0.8 copy-done.5
  3.0 0.7 copy-done.7
  3.7 1.0 shard_map.119
  4.8 27.5 %all_to_all.20.got_ref = f32[16,8,1152]{2,1,0:T(8,128)S(1)} all-to-all(f32[16,8,1152]{2,1,0:T(8,128)S(1)} %shard_map.119), channel_id=1, replica_groups=mesh['dp'=8,'zo'=4,'zi'=4,'cx'=4,'tensor'=2] {'zi','cx'}, dimensions={0} | all-to-all | bytes 1179648 | tf_op jit(solution)/shard_map/all_to_all | solution.py:321
  32.3 0.9 shard_map.120
  33.2 16.0 %all-to-all-start.1 = ((f32[4,8,1152]{2,1,0:T(8,128)}), f32[4,8,1152]{2,1,0:T(8,128)S(1)}, u32[]{:S(2)}, u32[]{:S(2)}) async-start(f32[4,8,1152]{2,1,0:T(8,128)} %shard_map.120), calls=%async_computation.1 | async-start | bytes 294912 | tf_op jit(solution)/shard_map/all_to_all | solution.py:351
  49.2 15.4 %all-to-all-done.1.totals_ref = f32[4,8,1152]{2,1,0:T(8,128)S(1)} async-done(((f32[4,8,1152]{2,1,0:T(8,128)}), f32[4,8,1152]{2,1,0:T(8,128)S(1)}, u32[]{:S(2)}, u32[]{:S(2)}) %all-to-all-start.1) | async-done | bytes 147488 | tf_op jit(solution)/shard_map/all_to_all | solution.py:351
  64.6 1.1 shard_map.121
  65.7 4.2 %all-to-all-start.2 = ((f32[16,8,1024]{2,1,0:T(8,128)}), f32[16,8,1024]{2,1,0:T(8,128)S(1)}, u32[]{:S(2)}, u32[]{:S(2)}) async-start(f32[16,8,1024]{2,1,0:T(8,128)} %shard_map.121), calls=%async_computation.2 | async-start | bytes 1048576 | tf_op jit(solution)/shard_map/all_to_all | solution.py:360
  69.9 4.5 %shard_map.122 = (f32[128,1024]{1,0:T(8,128)}, f32[128,1024]{1,0:T(8,128)}, bf16[128,1024]{1,0:T(8,128)(2,1)}, bf16[128,1024]{1,0:T(8,128)(2,1)}, f32[128,1024]{...) custom-call(bf16[128,1024]{1,0:T(8,128)(2,1)S(1)} %bitcast.16, ...), custom_call_target="tpu_custom_call" | custom-call | tf_op jit(solution)/shard_map/pallas_call | solution.py:296
  74.5 1.9 %collective-permute-start.1 = (f32[128,128]{1,0:T(8,128)S(1)}, f32[128,128]{1,0:T(8,128)S(1)}, u32[]{:S(2)}, u32[]{:S(2)}) collective-permute-start(f32[128,128]{1,0:T(8,128)S(1)} %get-tuple-element.36), channel_id=1, source_target_pairs={{0,1},{1,0},{2,3},{3,2},{4,5},{5,4},{6,7},{7,6},{8,9},{9,8},{10,11... | collective-permute-start | bytes 196616 | tf_op jit(solution)/shard_map/ppermute | solution.py:345
  76.4 6.6 %all-to-all-done.2.f_ref = f32[16,8,1024]{2,1,0:T(8,128)S(1)} async-done(((f32[16,8,1024]{2,1,0:T(8,128)}), f32[16,8,1024]{2,1,0:T(8,128)S(1)}, u32[]{:S(2)}, u32[]{:S(2)}) %all-to-all-start.2) | async-done | bytes 524320 | tf_op jit(solution)/shard_map/all_to_all | solution.py:360
  83.0 1.2 %shard_map.123.after_ref = f32[64,1,128]{2,1,0:T(1,128)} custom-call(f32[16,8,1024]{2,1,0:T(8,128)S(1)} %all-to-all-done.2.f_ref, f32[128,1024]{1,0:T(8,128)S(1)} %get-tuple-element.31.mt_ref, f32[1,128]{1,0:T(1,128)S(1)} %get-tuple-element.32.dr_ref), custom_call_target="tpu_custom_call" | custom-call | tf_op jit(solution)/shard_map/pallas_call | solution.py:296
  84.2 3.2 %shard_map.124 = (bf16[128,1024]{1,0:T(8,128)(2,1)}, f32[16,128]{1,0:T(8,128)}, f32[128,128]{1,0:T(8,128)S(1)}) custom-call(f32[16,8,1024]{2,1,0:T(8,128)S(1)} %all-to-all-done.2.f_ref, bf16[128,1024]{1,0:T(8,128)(2,1)S(1)} %bitcast.17, f32[16,128]{1,0:T(8,128)S(1)} %bitcast.27, bf16[128,128]{1,0:T(8,128)(2,1)S(1)} %bitcast.22, ...), custom_call_target="tpu_custom_call" | custom-call | tf_op jit(solution)/shard_map/pallas_call | solution.py:296
  87.4 1.9 %collective-permute-start = (f32[128,128]{1,0:T(8,128)S(1)}, f32[128,128]{1,0:T(8,128)S(1)}, u32[]{:S(2)}, u32[]{:S(2)}) collective-permute-start(f32[128,128]{1,0:T(8,128)S(1)} %get-tuple-element.35), channel_id=1, source_target_pairs={{0,1},{1,0},{2,3},{3,2},{4,5},{5,4},{6,7},{7,6},{8,9},{9,8},{10,11... | collective-permute-start | bytes 196616 | tf_op jit(solution)/shard_map/ppermute | solution.py:379
  89.3 0.0 collective-permute-done.1
  89.3 0.6 add_bitcast_fusion
  89.9 7.0 %all-to-all-start.3 = ((f32[64,1,128]{2,1,0:T(1,128)}), f32[64,1,128]{2,1,0:T(1,128)S(1)}, u32[]{:S(2)}, u32[]{:S(2)}) async-start(f32[64,1,128]{2,1,0:T(1,128)} %shard_map.123.after_ref), calls=%async_computation.3 | async-start | bytes 65536 | tf_op jit(solution)/shard_map/all_to_all | solution.py:368
  97.0 0.6 add_bitcast_fusion.1
  97.6 14.0 %all-to-all-done.3 = f32[64,1,128]{2,1,0:T(1,128)S(1)} async-done(((f32[64,1,128]{2,1,0:T(1,128)}), f32[64,1,128]{2,1,0:T(1,128)S(1)}, u32[]{:S(2)}, u32[]{:S(2)}) %all-to-all-start.3) | async-done | bytes 32800 | tf_op jit(solution)/shard_map/all_to_all | solution.py:368
  111.6 0.6 reduce_sum.11
  (18 shorter events, 0.0 us)
Async XLA Ops:
  0.6 0.7 copy-start.9
  0.6 0.7 copy-start.10
  1.3 0.9 copy-start.1
  2.3 0.8 copy-start.5
  3.0 0.7 copy-start.7
  33.2 31.4 %all-to-all-start.1 = ((f32[4,8,1152]{2,1,0:T(8,128)}), f32[4,8,1152]{2,1,0:T(8,128)S(1)}, u32[]{:S(2)}, u32[]{:S(2)}) async-start(f32[4,8,1152]{2,1,0:T(8,128)} %shard_map.120), calls=%async_computation.1 | async-start | bytes 294912 | tf_op jit(solution)/shard_map/all_to_all | solution.py:351
  64.6 5.3 %copy-start.4 = (bf16[1,128,128]{2,1,0:T(8,128)(2,1)S(1)}, bf16[1,128,128]{2,1,0:T(8,128)(2,1)}, u32[]{:S(2)}) copy-start(bf16[1,128,128]{2,1,0:T(8,128)(2,1)} %param.10) | copy-start | bytes 98308
  64.6 5.3 %copy-start.6 = (bf16[1,128,128]{2,1,0:T(8,128)(2,1)S(1)}, bf16[1,128,128]{2,1,0:T(8,128)(2,1)}, u32[]{:S(2)}) copy-start(bf16[1,128,128]{2,1,0:T(8,128)(2,1)} %param.11) | copy-start | bytes 98308
  64.6 5.3 %copy-start.8 = (f32[1,16,128]{2,1,0:T(8,128)S(1)}, f32[1,16,128]{2,1,0:T(8,128)}, u32[]{:S(2)}) copy-start(f32[1,16,128]{2,1,0:T(8,128)} %param.9) | copy-start | bytes 24580
  65.7 4.2 %copy-start = (bf16[1,128,1024]{2,1,0:T(8,128)(2,1)S(1)}, bf16[1,128,1024]{2,1,0:T(8,128)(2,1)}, u32[]{:S(2)}) copy-start(bf16[1,128,1024]{2,1,0:T(8,128)(2,1)} %param.8) | copy-start | bytes 786436
  65.7 4.3 %copy-start.2 = (bf16[1,128,1024]{2,1,0:T(8,128)(2,1)S(1)}, bf16[1,128,1024]{2,1,0:T(8,128)(2,1)}, u32[]{:S(2)}) copy-start(bf16[1,128,1024]{2,1,0:T(8,128)(2,1)} %param.12) | copy-start | bytes 786436
  65.7 4.3 %copy-start.3 = (f32[1,1,1024,128]{3,2,1,0:T(8,128)S(1)}, f32[1,1,1024,128]{3,2,1,0:T(8,128)}, u32[]{:S(2)}) copy-start(f32[1,1,1024,128]{3,2,1,0:T(8,128)} %param.13) | copy-start | bytes 1572868
  65.7 17.3 %all-to-all-start.2 = ((f32[16,8,1024]{2,1,0:T(8,128)}), f32[16,8,1024]{2,1,0:T(8,128)S(1)}, u32[]{:S(2)}, u32[]{:S(2)}) async-start(f32[16,8,1024]{2,1,0:T(8,128)} %shard_map.121), calls=%async_computation.2 | async-start | bytes 1048576 | tf_op jit(solution)/shard_map/all_to_all | solution.py:360
  74.5 14.8 %collective-permute-start.1 = (f32[128,128]{1,0:T(8,128)S(1)}, f32[128,128]{1,0:T(8,128)S(1)}, u32[]{:S(2)}, u32[]{:S(2)}) collective-permute-start(f32[128,128]{1,0:T(8,128)S(1)} %get-tuple-element.36), channel_id=1, source_target_pairs={{0,1},{1,0},{2,3},{3,2},{4,5},{5,4},{6,7},{7,6},{8,9},{9,8},{10,11... | collective-permute-start | bytes 196616 | tf_op jit(solution)/shard_map/ppermute | solution.py:345
  87.4 9.6 %collective-permute-start = (f32[128,128]{1,0:T(8,128)S(1)}, f32[128,128]{1,0:T(8,128)S(1)}, u32[]{:S(2)}, u32[]{:S(2)}) collective-permute-start(f32[128,128]{1,0:T(8,128)S(1)} %get-tuple-element.35), channel_id=1, source_target_pairs={{0,1},{1,0},{2,3},{3,2},{4,5},{5,4},{6,7},{7,6},{8,9},{9,8},{10,11... | collective-permute-start | bytes 196616 | tf_op jit(solution)/shard_map/ppermute | solution.py:379
  89.9 21.7 %all-to-all-start.3 = ((f32[64,1,128]{2,1,0:T(1,128)}), f32[64,1,128]{2,1,0:T(1,128)S(1)}, u32[]{:S(2)}, u32[]{:S(2)}) async-start(f32[64,1,128]{2,1,0:T(1,128)} %shard_map.123.after_ref), calls=%async_computation.3 | async-start | bytes 65536 | tf_op jit(solution)/shard_map/all_to_all | solution.py:368

commit v3 on v2

--- a/solution.py
+++ b/solution.py
@@ -200,9 +200,11 @@
     part = f_ref[0] * mt_ref[:rows, :]
     for k in range(1, n // rows):
         part = part + f_ref[k] * mt_ref[k * rows : (k + 1) * rows, :]
-    hot = head_rows(LANES, width, head_dim)
-    each = mmt_exact(part, hot.astype(F32))
-    out = dr_ref[...] - jnp.sum(each, axis=0, keepdims=True)
+    heads = width // head_dim
+    hot = head_rows(heads, width, head_dim)
+    each = jnp.sum(mmt_exact(hot.astype(F32), part), axis=1, keepdims=True)
+    diag = iota((heads, LANES), 0) == iota((heads, LANES), 1)
+    out = dr_ref[...] - jnp.sum(jnp.where(diag, each, 0.0), axis=0, keepdims=True)
     out_ref[...] = jnp.broadcast_to(out.reshape(1, 1, LANES), (ctx, 1, LANES))
 
 
@@ -317,7 +319,12 @@
     x, dt, b, c, dy = (a[0] for a in (x_seq, dt_seq, b_seq, c_seq, dy_seq))
     h = saved_states[0, 0]
     rates = decay_rates[None]
-    (acc,) = call(acc_kernel, [((near, rows, width + LANES), F32)], dy, dt, c, doc_starts, rates)
+    (acc,) = call(
+        acc_kernel,
+        [((near, rows, width + LANES), F32)],
+        *(dy, dt, c, doc_starts, rates),
+        far=range(5),
+    )
     got = lax.all_to_all(acc, ("zi", "cx"), 0, 0)
     wide, small, square, state = (tok, width), (heads, tok), (tok, n), (n, width)
     local = call(

time: 113 us -> 111 us (0.982)
  local copies, waits for them, and re-layouts: 3.08 us -> 0.62 us
    unnamed x22 -> x16, local copies, waits for them, and re-layouts: 3.08 us -> 0.62 us
where the time goes in v3:
time: 111 us; the launch traced here: 110 us
  waiting for transfers between devices  35.5 us (32%)
  starting transfers between devices  31.1 us (28%)
  blocking collectives  27.5 us (25%)
  Pallas kernels  12.7 us (11%)
  other arithmetic  1.87 us (2%)
    all_to_all x1, blocking collectives, per_device(): got = lax.all_to_all(acc, ('zi', 'cx'), 0, 0)  27.5 us
    all_to_all x1, starting transfers between devices, per_device(): spread = lax.all_to_all(total, 'zo', 0, 0)  16 us
    all_to_all x1, waiting for transfers between devices, per_device(): spread = lax.all_to_all(total, 'zo', 0, 0)  15.4 us
    all_to_all x1, waiting for transfers between devices, per_device(): dr_parts = lax.all_to_all(dr_all, ('zo', 'zi', 'cx'), 0, 0)  14.1 us
    pallas_call x6, Pallas kernels, call(): pl.pallas_call(kernel, out_shape=shapes, in_specs=[smem] * scalars + [vme...  12.7 us
    all_to_all x1, starting transfers between devices, per_device(): dr_parts = lax.all_to_all(dr_all, ('zo', 'zi', 'cx'), 0, 0)  7.01 us
    all_to_all x1, waiting for transfers between devices, per_device(): incoming = lax.all_to_all(carry, ('zi', 'cx'), 0, 0)  5.99 us
    all_to_all x1, starting transfers between devices, per_device(): incoming = lax.all_to_all(carry, ('zi', 'cx'), 0, 0)  4.2 us
  transfers between devices with their start and end apart: 5, of which 3 were waited for; matrix products, arithmetic and copies ran while one was open for 1% of the time, Pallas kernels for 8%

profile of v3, /device:TPU:56, one launch (start us, length us, event | category | flops | bytes accessed | tf_op | source)
XLA Modules:
  0.0 110.0 jit_solution(403749952148722407)
XLA Ops:
  0.6 2.0 %shard_map.119 = f32[16,8,1152]{2,1,0:T(8,128)S(1)} custom-call(bf16[128,1024]{1,0:T(8,128)(2,1)} %bitcast.18, f32[16,128]{1,0:T(8,128)} %bitcast.25, bf16[128,128]{1,0:T(8,128)(2,1)} %bitcast.23, s32[1,128]{1,0:T(1,128)} %st_ref.3, f32[1,16]{1,0:T(1,128)} %bitcast.28), custom_call_target="tpu_custom_call" | custom-call | tf_op jit(solution)/shard_map/pallas_call | solution.py:298
  2.7 27.5 %all_to_all.20.got_ref = f32[16,8,1152]{2,1,0:T(8,128)S(1)} all-to-all(f32[16,8,1152]{2,1,0:T(8,128)S(1)} %shard_map.119), channel_id=1, replica_groups=mesh['dp'=8,'zo'=4,'zi'=4,'cx'=4,'tensor'=2] {'zi','cx'}, dimensions={0} | all-to-all | bytes 1179648 | tf_op jit(solution)/shard_map/all_to_all | solution.py:328
  30.2 0.9 shard_map.120
  31.1 16.0 %all-to-all-start.1 = ((f32[4,8,1152]{2,1,0:T(8,128)}), f32[4,8,1152]{2,1,0:T(8,128)S(1)}, u32[]{:S(2)}, u32[]{:S(2)}) async-start(f32[4,8,1152]{2,1,0:T(8,128)} %shard_map.120), calls=%async_computation.1 | async-start | bytes 294912 | tf_op jit(solution)/shard_map/all_to_all | solution.py:358
  47.1 15.4 %all-to-all-done.1.totals_ref = f32[4,8,1152]{2,1,0:T(8,128)S(1)} async-done(((f32[4,8,1152]{2,1,0:T(8,128)}), f32[4,8,1152]{2,1,0:T(8,128)S(1)}, u32[]{:S(2)}, u32[]{:S(2)}) %all-to-all-start.1) | async-done | bytes 147488 | tf_op jit(solution)/shard_map/all_to_all | solution.py:358
  62.5 1.1 shard_map.121
  63.6 4.2 %all-to-all-start.2 = ((f32[16,8,1024]{2,1,0:T(8,128)}), f32[16,8,1024]{2,1,0:T(8,128)S(1)}, u32[]{:S(2)}, u32[]{:S(2)}) async-start(f32[16,8,1024]{2,1,0:T(8,128)} %shard_map.121), calls=%async_computation.2 | async-start | bytes 1048576 | tf_op jit(solution)/shard_map/all_to_all | solution.py:367
  67.8 0.0 copy-start.6
  67.8 0.0 copy-start.7
  67.9 0.6 copy-done.6
  68.5 0.0 copy-done.7
  68.5 4.5 %shard_map.122 = (f32[128,1024]{1,0:T(8,128)}, f32[128,1024]{1,0:T(8,128)}, bf16[128,1024]{1,0:T(8,128)(2,1)}, bf16[128,1024]{1,0:T(8,128)(2,1)}, f32[128,1024]{...) custom-call(bf16[128,1024]{1,0:T(8,128)(2,1)S(1)} %bitcast.16, ...), custom_call_target="tpu_custom_call" | custom-call | tf_op jit(solution)/shard_map/pallas_call | solution.py:298
  73.0 1.9 %collective-permute-start.1 = (f32[128,128]{1,0:T(8,128)S(1)}, f32[128,128]{1,0:T(8,128)S(1)}, u32[]{:S(2)}, u32[]{:S(2)}) collective-permute-start(f32[128,128]{1,0:T(8,128)S(1)} %get-tuple-element.36), channel_id=1, source_target_pairs={{0,1},{1,0},{2,3},{3,2},{4,5},{5,4},{6,7},{7,6},{8,9},{9,8},{10,11... | collective-permute-start | bytes 196616 | tf_op jit(solution)/shard_map/ppermute | solution.py:352
  74.9 6.0 %all-to-all-done.2.f_ref = f32[16,8,1024]{2,1,0:T(8,128)S(1)} async-done(((f32[16,8,1024]{2,1,0:T(8,128)}), f32[16,8,1024]{2,1,0:T(8,128)S(1)}, u32[]{:S(2)}, u32[]{:S(2)}) %all-to-all-start.2) | async-done | bytes 524320 | tf_op jit(solution)/shard_map/all_to_all | solution.py:367
  80.9 1.0 shard_map.123.after_ref
  81.9 3.2 %shard_map.124 = (bf16[128,1024]{1,0:T(8,128)(2,1)}, f32[16,128]{1,0:T(8,128)}, f32[128,128]{1,0:T(8,128)S(1)}) custom-call(f32[16,8,1024]{2,1,0:T(8,128)S(1)} %all-to-all-done.2.f_ref, bf16[128,1024]{1,0:T(8,128)(2,1)S(1)} %bitcast.17, f32[16,128]{1,0:T(8,128)S(1)} %bitcast.27, bf16[128,128]{1,0:T(8,128)(2,1)S(1)} %bitcast.22, ...), custom_call_target="tpu_custom_call" | custom-call | tf_op jit(solution)/shard_map/pallas_call | solution.py:298
  85.1 1.9 %collective-permute-start = (f32[128,128]{1,0:T(8,128)S(1)}, f32[128,128]{1,0:T(8,128)S(1)}, u32[]{:S(2)}, u32[]{:S(2)}) collective-permute-start(f32[128,128]{1,0:T(8,128)S(1)} %get-tuple-element.35), channel_id=1, source_target_pairs={{0,1},{1,0},{2,3},{3,2},{4,5},{5,4},{6,7},{7,6},{8,9},{9,8},{10,11... | collective-permute-start | bytes 196616 | tf_op jit(solution)/shard_map/ppermute | solution.py:386
  87.0 0.0 collective-permute-done.1
  87.0 0.6 add_bitcast_fusion
  87.6 7.0 %all-to-all-start.3 = ((f32[64,1,128]{2,1,0:T(1,128)}), f32[64,1,128]{2,1,0:T(1,128)S(1)}, u32[]{:S(2)}, u32[]{:S(2)}) async-start(f32[64,1,128]{2,1,0:T(1,128)} %shard_map.123.after_ref), calls=%async_computation.3 | async-start | bytes 65536 | tf_op jit(solution)/shard_map/all_to_all | solution.py:375
  94.7 0.0 collective-permute-done
  94.7 0.6 add_bitcast_fusion.1
  95.3 14.1 %all-to-all-done.3 = f32[64,1,128]{2,1,0:T(1,128)S(1)} async-done(((f32[64,1,128]{2,1,0:T(1,128)}), f32[64,1,128]{2,1,0:T(1,128)S(1)}, u32[]{:S(2)}, u32[]{:S(2)}) %all-to-all-start.3) | async-done | bytes 32800 | tf_op jit(solution)/shard_map/all_to_all | solution.py:375
  109.4 0.6 reduce_sum.11
  (12 shorter events, 0.0 us)
Async XLA Ops:
  31.1 31.4 %all-to-all-start.1 = ((f32[4,8,1152]{2,1,0:T(8,128)}), f32[4,8,1152]{2,1,0:T(8,128)S(1)}, u32[]{:S(2)}, u32[]{:S(2)}) async-start(f32[4,8,1152]{2,1,0:T(8,128)} %shard_map.120), calls=%async_computation.1 | async-start | bytes 294912 | tf_op jit(solution)/shard_map/all_to_all | solution.py:358
  62.5 5.3 %copy-start.3 = (bf16[1,128,128]{2,1,0:T(8,128)(2,1)S(1)}, bf16[1,128,128]{2,1,0:T(8,128)(2,1)}, u32[]{:S(2)}) copy-start(bf16[1,128,128]{2,1,0:T(8,128)(2,1)} %param.10) | copy-start | bytes 98308
  62.5 5.3 %copy-start.4 = (bf16[1,128,128]{2,1,0:T(8,128)(2,1)S(1)}, bf16[1,128,128]{2,1,0:T(8,128)(2,1)}, u32[]{:S(2)}) copy-start(bf16[1,128,128]{2,1,0:T(8,128)(2,1)} %param.11) | copy-start | bytes 98308
  62.5 5.4 %copy-start.5 = (f32[1,16,128]{2,1,0:T(8,128)S(1)}, f32[1,16,128]{2,1,0:T(8,128)}, u32[]{:S(2)}) copy-start(f32[1,16,128]{2,1,0:T(8,128)} %param.9) | copy-start | bytes 24580
  63.6 4.3 %copy-start = (bf16[1,128,1024]{2,1,0:T(8,128)(2,1)S(1)}, bf16[1,128,1024]{2,1,0:T(8,128)(2,1)}, u32[]{:S(2)}) copy-start(bf16[1,128,1024]{2,1,0:T(8,128)(2,1)} %param.8) | copy-start | bytes 786436
  63.6 4.3 %copy-start.1 = (bf16[1,128,1024]{2,1,0:T(8,128)(2,1)S(1)}, bf16[1,128,1024]{2,1,0:T(8,128)(2,1)}, u32[]{:S(2)}) copy-start(bf16[1,128,1024]{2,1,0:T(8,128)(2,1)} %param.12) | copy-start | bytes 786436
  63.6 4.3 %copy-start.2 = (f32[1,1,1024,128]{3,2,1,0:T(8,128)S(1)}, f32[1,1,1024,128]{3,2,1,0:T(8,128)}, u32[]{:S(2)}) copy-start(f32[1,1,1024,128]{3,2,1,0:T(8,128)} %param.13) | copy-start | bytes 1572868
  63.6 17.3 %all-to-all-start.2 = ((f32[16,8,1024]{2,1,0:T(8,128)}), f32[16,8,1024]{2,1,0:T(8,128)S(1)}, u32[]{:S(2)}, u32[]{:S(2)}) async-start(f32[16,8,1024]{2,1,0:T(8,128)} %shard_map.121), calls=%async_computation.2 | async-start | bytes 1048576 | tf_op jit(solution)/shard_map/all_to_all | solution.py:367
  67.8 0.7 copy-start.6
  67.8 0.7 copy-start.7
  73.0 14.0 %collective-permute-start.1 = (f32[128,128]{1,0:T(8,128)S(1)}, f32[128,128]{1,0:T(8,128)S(1)}, u32[]{:S(2)}, u32[]{:S(2)}) collective-permute-start(f32[128,128]{1,0:T(8,128)S(1)} %get-tuple-element.36), channel_id=1, source_target_pairs={{0,1},{1,0},{2,3},{3,2},{4,5},{5,4},{6,7},{7,6},{8,9},{9,8},{10,11... | collective-permute-start | bytes 196616 | tf_op jit(solution)/shard_map/ppermute | solution.py:352
  85.1 9.6 %collective-permute-start = (f32[128,128]{1,0:T(8,128)S(1)}, f32[128,128]{1,0:T(8,128)S(1)}, u32[]{:S(2)}, u32[]{:S(2)}) collective-permute-start(f32[128,128]{1,0:T(8,128)S(1)} %get-tuple-element.35), channel_id=1, source_target_pairs={{0,1},{1,0},{2,3},{3,2},{4,5},{5,4},{6,7},{7,6},{8,9},{9,8},{10,11... | collective-permute-start | bytes 196616 | tf_op jit(solution)/shard_map/ppermute | solution.py:386
  87.6 21.8 %all-to-all-start.3 = ((f32[64,1,128]{2,1,0:T(1,128)}), f32[64,1,128]{2,1,0:T(1,128)S(1)}, u32[]{:S(2)}, u32[]{:S(2)}) async-start(f32[64,1,128]{2,1,0:T(1,128)} %shard_map.123.after_ref), calls=%async_computation.3 | async-start | bytes 65536 | tf_op jit(solution)/shard_map/all_to_all | solution.py:375
